TPU v7x, 32 devices: a whole 2x2x4 slice. The times are simulated.
32 devices in a mesh: row: 8 (over z, x), col: 4 (over y, core).
Axes of the slice: x: 2, y: 2, z: 4, core: 2. Of those that a mesh axis runs over, the one named last changes fastest.
Arguments:
- tokens: bfloat16 [4096, 768], P(('row', 'col')), may hold values from -6 to 6
- w_qkv: bfloat16 [768, 3, 768], P('row', None, 'col'), may hold values from -0.21875 to 0.21875
- w_out: bfloat16 [768, 768], P('col', 'row'), may hold values from -2.5 to 2.5
- w_gate_up: bfloat16 [768, 2, 3072], P('row', None, 'col'), may hold values from -0.21875 to 0.21875
- w_down: bfloat16 [3072, 768], P('col', 'row'), may hold values from -0.109375 to 0.109375
- gain1: float32 [768], replicated, may hold values from 0.1 to 1.9
- bias1: float32 [768], replicated, may hold values from -1.8 to 1.8
- gain2: float32 [768], replicated, may hold values from 0.1 to 1.9
- bias2: float32 [768], replicated, may hold values from -1.8 to 1.8
- cotangent: bfloat16 [4096, 768], P(('row', 'col')), may hold values from -6 to 6
- seq_lengths: int32 [3], replicated, may hold values from 512 to 2048, as said below
- packed_order: int32 [4096], replicated, may hold values from 0 to 4095, each once
Outputs:
- output: bfloat16 [4096, 768], P(('row', 'col'))
- grad_tokens: float32 [4096, 768], P(('row', 'col'))
- grad_w_qkv: float32 [768, 3, 768], P('row', None, 'col')
- grad_w_out: float32 [768, 768], P('col', 'row')
- grad_w_gate_up: float32 [768, 2, 3072], P('row', None, 'col')
- grad_w_down: float32 [3072, 768], P('col', 'row')
- grad_gain1: float32 [768], replicated
- grad_bias1: float32 [768], replicated
- grad_gain2: float32 [768], replicated
- grad_bias2: float32 [768], replicated
Inputs may be any that keep to these rules, and one draw needn't show every extreme that they name: `seq_lengths`: 3 lengths that sum to 4096; the longest is exactly 2048.
All inputs are finite; a program needn't handle non-finite values.
Results may differ from a plain program's by a relative error of at most 0.024.
Values may be sent and summed in bfloat16 or wider, within the bound.
No kernel may reach another device: no remote copies, remote signals or barrier semaphores. Data moves between devices by JAX's collectives and lax.ppermute only.
A program may use at most 512 MiB of HBM per device.

v0:
```python
import math
import jax
import jax.numpy as jnp
from jax import lax
from jax.sharding import PartitionSpec as P

HEAD = 64
ROPE_BASE = 1000.0
NORM_EPS = 1e-12
MASKED = -1e30


def token_layout(seq_lengths, packed_order):
    seq_ends = jnp.cumsum(seq_lengths)
    seq_starts = seq_ends - seq_lengths
    seq_id = jnp.sum((packed_order[:, None] >= seq_ends[None, :]).astype(jnp.int32), axis=1)
    member = seq_id[:, None] == jnp.arange(seq_lengths.shape[0], dtype=jnp.int32)[None, :]
    start_of = jnp.sum(jnp.where(member, seq_starts[None, :], 0), axis=1)
    return (seq_id, packed_order - start_of)


def rope_tables(positions, head):
    half = head // 2
    freqs = ROPE_BASE ** (-jnp.arange(half, dtype=jnp.float32) * 2.0 / head)
    angles = positions.astype(jnp.float32)[:, None] * freqs[None, :]
    return (jnp.cos(angles), jnp.sin(angles))


def rotate(field, cosine, sine):
    half = field.shape[-1] // 2
    first = field[..., :half]
    second = field[..., half:]
    cos_b = cosine[:, None, :]
    sin_b = sine[:, None, :]
    return jnp.concatenate(
        [first * cos_b - second * sin_b, second * cos_b + first * sin_b], axis=-1
    )


def rotate_back(field, cosine, sine):
    half = field.shape[-1] // 2
    first = field[..., :half]
    second = field[..., half:]
    cos_b = cosine[:, None, :]
    sin_b = sine[:, None, :]
    return jnp.concatenate(
        [first * cos_b + second * sin_b, second * cos_b - first * sin_b], axis=-1
    )


def norm_forward(values, gain, bias):
    centered = values - jnp.mean(values, axis=-1, keepdims=True)
    inverse = lax.rsqrt(jnp.mean(centered * centered, axis=-1, keepdims=True) + NORM_EPS)
    normed = centered * inverse
    return (normed * gain + bias, normed, inverse)


def norm_backward(grad_out, normed, inverse, gain):
    scaled = grad_out * gain
    grad_in = inverse * (
        scaled
        - jnp.mean(scaled, axis=-1, keepdims=True)
        - normed * jnp.mean(scaled * normed, axis=-1, keepdims=True)
    )
    return (grad_in, jnp.sum(grad_out * normed, axis=0), jnp.sum(grad_out, axis=0))


def gather_rows(rows):
    return lax.all_gather(rows, "col", axis=0, tiled=True)


def gather_grads(rows):
    return lax.all_gather(rows, "col", axis=0, tiled=True)


def column_sum(left, product):
    return lax.psum_scatter(
        product(left).astype(jnp.bfloat16), "col", scatter_dimension=0, tiled=True
    ).astype(jnp.float32)


def score_block(queries, seg_queries, key_rows, seg_keys, scale):
    count = key_rows.shape[0]
    heads = queries.shape[1]
    head = queries.shape[2]
    scores = (
        jnp.einsum(
            "qhd,khd->hqk",
            queries,
            key_rows.reshape(count, heads, head),
            preferred_element_type=jnp.float32,
        )
        * scale
    )
    same = seg_queries[:, None] == seg_keys[None, :]
    return (scores, same)


def probabilities(queries, seg_queries, log_total, key_rows, seg_keys, scale):
    scores, same = score_block(queries, seg_queries, key_rows, seg_keys, scale)
    return jnp.where(same[None], jnp.exp(scores - log_total[..., None]), 0.0)


def score_grads(probs, grad_heads, delta, value_rows):
    count = value_rows.shape[0]
    heads = grad_heads.shape[1]
    head = grad_heads.shape[2]
    grad_probs = jnp.einsum(
        "qhd,khd->hqk",
        grad_heads,
        value_rows.reshape(count, heads, head),
        preferred_element_type=jnp.float32,
    )
    return (probs * (grad_probs - delta[..., None])).astype(jnp.bfloat16)


def local(
    tokens,
    w_qkv,
    w_out,
    w_gate_up,
    w_down,
    gain1,
    bias1,
    gain2,
    bias2,
    cotangent,
    seq_lengths,
    packed_order,
):
    row_index = lax.axis_index("row")
    shards = lax.axis_size("row")
    full_qkv, full_out, full_gate_up, full_down = (
        lax.all_gather(w_qkv, "row", axis=0, tiled=True),
        lax.all_gather(w_out, "row", axis=1, tiled=True),
        lax.all_gather(w_gate_up, "row", axis=0, tiled=True),
        lax.all_gather(w_down, "row", axis=1, tiled=True),
    )
    seq_all, positions = token_layout(seq_lengths, packed_order)
    token_block = gather_rows(tokens)
    group = token_block.shape[0]
    first_slot = row_index * group
    seg_rows = lax.dynamic_slice_in_dim(seq_all, first_slot, group, 0)
    cosine, sine = rope_tables(lax.dynamic_slice_in_dim(positions, first_slot, group, 0), HEAD)
    width = full_qkv.shape[2]
    local_heads = width // HEAD
    scale = 1.0 / math.sqrt(HEAD)
    mixed = jnp.einsum("td,dce->tce", token_block, full_qkv, preferred_element_type=jnp.float32)
    query_bf = rotate(mixed[:, 0].reshape(group, local_heads, HEAD), cosine, sine).astype(
        jnp.bfloat16
    )
    key_bf = (
        rotate(mixed[:, 1].reshape(group, local_heads, HEAD), cosine, sine)
        .astype(jnp.bfloat16)
        .reshape(group, width)
    )
    value_bf = mixed[:, 2].astype(jnp.bfloat16)
    run_max = jnp.full((local_heads, group), MASKED, jnp.float32)
    key_piece = lax.all_gather(key_bf, "row", axis=0, tiled=True)
    value_piece = lax.all_gather(value_bf, "row", axis=0, tiled=True)
    count = key_piece.shape[0]
    seg_keys = seq_all
    scores, same = score_block(query_bf, seg_rows, key_piece, seg_keys, scale)
    new_max = jnp.maximum(run_max, jnp.max(jnp.where(same[None], scores, MASKED), axis=-1))
    weights_now = jnp.where(same[None], jnp.exp(scores - new_max[..., None]), 0.0)
    new_total = jnp.sum(weights_now, axis=-1)
    new_acc = jnp.einsum(
        "hqk,khd->hqd",
        weights_now.astype(jnp.bfloat16),
        value_piece.reshape(count, local_heads, HEAD),
        preferred_element_type=jnp.float32,
    )
    context = new_acc / new_total[..., None]
    log_total = new_max + jnp.log(new_total)
    context_bf = jnp.transpose(context, (1, 0, 2)).reshape(group, width).astype(jnp.bfloat16)

    def out_product(rows):
        return jnp.dot(rows, full_out, preferred_element_type=jnp.float32)

    attn_out = column_sum(context_bf, out_product)
    residual1 = tokens.astype(jnp.float32) + attn_out
    hidden1, normed1, inverse1 = norm_forward(residual1, gain1, bias1)
    hidden_block = gather_rows(hidden1.astype(jnp.bfloat16))
    gate_up = jnp.einsum(
        "td,dcf->tcf", hidden_block, full_gate_up, preferred_element_type=jnp.float32
    )
    up = gate_up[:, 0]
    gate = gate_up[:, 1]
    sigma = jax.nn.sigmoid(gate)
    inner = (gate * sigma * up).astype(jnp.bfloat16)

    def down_product(rows):
        return jnp.dot(rows, full_down, preferred_element_type=jnp.float32)

    ffn_out = column_sum(inner, down_product)
    residual2 = hidden1 + ffn_out
    result, normed2, inverse2 = norm_forward(residual2, gain2, bias2)
    grad_res2, grad_gain2, grad_bias2 = norm_backward(
        cotangent.astype(jnp.float32), normed2, inverse2, gain2
    )
    grad_ffn = gather_grads(grad_res2.astype(jnp.bfloat16))
    grad_inner = lax.dot_general(
        grad_ffn, full_down, (((1,), (1,)), ((), ())), preferred_element_type=jnp.float32
    )
    grad_down = lax.dot_general(
        inner, grad_ffn, (((0,), (0,)), ((), ())), preferred_element_type=jnp.float32
    )
    grad_up = grad_inner * gate * sigma
    grad_gate = grad_inner * up * sigma * (1.0 + gate * (1.0 - sigma))
    grad_gate_up = jnp.stack([grad_up, grad_gate], axis=1).astype(jnp.bfloat16)

    def gate_up_back(rows):
        return jnp.einsum("tcf,dcf->td", rows, full_gate_up, preferred_element_type=jnp.float32)

    grad_hidden1 = grad_res2 + column_sum(grad_gate_up, gate_up_back)
    grad_wgu = jnp.einsum(
        "td,tcf->dcf", hidden_block, grad_gate_up, preferred_element_type=jnp.float32
    )
    grad_res1, grad_gain1, grad_bias1 = norm_backward(grad_hidden1, normed1, inverse1, gain1)
    grad_attn = gather_grads(grad_res1.astype(jnp.bfloat16))
    grad_wo = lax.dot_general(
        context_bf, grad_attn, (((0,), (0,)), ((), ())), preferred_element_type=jnp.float32
    )
    grad_context_bf = lax.dot_general(
        grad_attn, full_out, (((1,), (1,)), ((), ())), preferred_element_type=jnp.float32
    ).astype(jnp.bfloat16)
    grad_heads = grad_context_bf.reshape(group, local_heads, HEAD)
    delta = jnp.sum(jnp.transpose(grad_heads, (1, 0, 2)).astype(jnp.float32) * context, axis=-1)
    key_all, value_all = (
        lax.all_gather(key_bf, "row", axis=0, tiled=True),
        lax.all_gather(value_bf, "row", axis=0, tiled=True),
    )
    tokens_total = key_all.shape[0]
    per_turn = group * math.gcd(shards, max(1, 2048 // group))
    turns = tokens_total // per_turn

    def turn_terms(turn):
        begin = turn * per_turn
        key_rows = lax.dynamic_slice_in_dim(key_all, begin, per_turn, 0)
        value_rows = lax.dynamic_slice_in_dim(value_all, begin, per_turn, 0)
        seg_keys = lax.dynamic_slice_in_dim(seq_all, begin, per_turn, 0)
        probs = probabilities(query_bf, seg_rows, log_total, key_rows, seg_keys, scale)
        grad_scores = score_grads(probs, grad_heads, delta, value_rows)
        return (begin, key_rows, probs, grad_scores)

    def query_term(grad_scores, key_rows):
        return jnp.einsum(
            "hqk,khd->qhd",
            grad_scores,
            key_rows.reshape(per_turn, local_heads, HEAD),
            preferred_element_type=jnp.float32,
        )

    empty_query = jnp.zeros((group, local_heads, HEAD), jnp.float32)

    def key_turn(turn, carry):
        grad_query, grad_keys, grad_values = carry
        begin, key_rows, probs, grad_scores = turn_terms(turn)
        grad_query = grad_query + query_term(grad_scores, key_rows)
        key_term = jnp.einsum(
            "hqk,qhd->khd", grad_scores, query_bf, preferred_element_type=jnp.float32
        ).reshape(per_turn, width)
        value_term = jnp.einsum(
            "hqk,qhd->khd",
            probs.astype(jnp.bfloat16),
            grad_heads,
            preferred_element_type=jnp.float32,
        ).reshape(per_turn, width)
        grad_keys = lax.dynamic_update_slice_in_dim(grad_keys, key_term, begin, 0)
        grad_values = lax.dynamic_update_slice_in_dim(grad_values, value_term, begin, 0)
        return (grad_query, grad_keys, grad_values)

    empty_keys = jnp.zeros((tokens_total, width), jnp.float32)
    grad_query, grad_keys_all, grad_values_all = lax.fori_loop(
        0, turns, key_turn, (empty_query, empty_keys, empty_keys)
    )
    grad_key_rows, grad_value_rows = (
        lax.psum_scatter(grad_keys_all, "row", scatter_dimension=0, tiled=True),
        lax.psum_scatter(grad_values_all, "row", scatter_dimension=0, tiled=True),
    )
    grad_query_raw = rotate_back(grad_query * scale, cosine, sine).reshape(group, width)
    grad_key_raw = rotate_back(
        grad_key_rows.reshape(group, local_heads, HEAD) * scale, cosine, sine
    ).reshape(group, width)
    grad_mixed = jnp.stack([grad_query_raw, grad_key_raw, grad_value_rows], axis=1).astype(
        jnp.bfloat16
    )

    def qkv_back(rows):
        return jnp.einsum("tce,dce->td", rows, full_qkv, preferred_element_type=jnp.float32)

    grad_tokens = grad_res1 + column_sum(grad_mixed, qkv_back)
    grad_wqkv = jnp.einsum(
        "td,tce->dce", token_block, grad_mixed, preferred_element_type=jnp.float32
    )
    grad_w_qkv, grad_w_out, grad_w_gate_up, grad_w_down = (
        lax.psum_scatter(grad_wqkv, "row", scatter_dimension=0, tiled=True),
        lax.psum_scatter(grad_wo, "row", scatter_dimension=1, tiled=True),
        lax.psum_scatter(grad_wgu, "row", scatter_dimension=0, tiled=True),
        lax.psum_scatter(grad_down, "row", scatter_dimension=1, tiled=True),
    )
    norm_gain1, norm_bias1, norm_gain2, norm_bias2 = lax.psum(
        (grad_gain1, grad_bias1, grad_gain2, grad_bias2), ("row", "col")
    )
    return (
        result.astype(jnp.bfloat16),
        grad_tokens,
        grad_w_qkv,
        grad_w_out,
        grad_w_gate_up,
        grad_w_down,
        norm_gain1,
        norm_bias1,
        norm_gain2,
        norm_bias2,
    )


def solution(mesh):
    placed = (
        P(("row", "col"), None),
        P("row", None, "col"),
        P("col", "row"),
        P("row", None, "col"),
        P("col", "row"),
        P(),
        P(),
        P(),
        P(),
        P(("row", "col"), None),
        P(),
        P(),
    )
    return jax.shard_map(
        local,
        mesh=mesh,
        in_specs=placed,
        out_specs=(
            P(("row", "col"), None),
            P(("row", "col"), None),
            P("row", None, "col"),
            P("col", "row"),
            P("row", None, "col"),
            P("col", "row"),
            P(),
            P(),
            P(),
            P(),
        ),
        check_vma=False,
    )
```

profile of v0, /device:TPU:0, one launch (start us, length us, event | category | flops | bytes accessed | tf_op | source)
XLA Modules:
  0.0 918.4 jit_solution(15256059629411682818)
XLA Ops:
  9.8 38.8 %all_gather.33 = bf16[768,3,192]{2,1,0:T(4,128)(2,1)S(1)} all-gather(bf16[96,3,192]{2,1,0:T(4,128)(2,1)S(1)} %copy.45), channel_id=1, replica_groups=mesh['row'=8,'col'=4] {'row'}, dimensions={0}, use_global_device_ids=true | all-gather | bytes 995328 | tf_op jit(solution)/shard_map/all_gather | solution.py:134
  49.5 8.8 all_gather.32
  64.3 31.8 %all_gather.36 = bf16[192,768]{0,1:T(8,128)(2,1)S(1)} all-gather(bf16[192,96]{0,1:T(8,128)(2,1)S(1)} %copy.47), channel_id=1, replica_groups=mesh['row'=8,'col'=4] {'row'}, dimensions={1}, use_global_device_ids=true | all-gather | bytes 331776 | tf_op jit(solution)/shard_map/all_gather | solution.py:135
  96.1 11.8 %all-gather.6.cloned.1.call-done = bf16[4096,192]{0,1:T(8,128)(2,1)} async-done(((bf16[512,192]{0,1:T(8,128)(2,1)}), bf16[4096,192]{0,1:T(8,128)(2,1)}) %all-gather.6.cloned.1.call-update) | async-done | bytes 1572880 | tf_op jit(solution)/shard_map/all_gather | solution.py:159
  107.9 12.5 %select_reduce_fusion = (f32[3,512]{1,0:T(4,128)S(1)}, f32[3,512,4096]{2,1,0:T(8,128)}) fusion(pred[512,4096]{1,0:T(8,128)(4,1)S(1)} %broadcast_compare_fusion.1, bf16[4096,3,64]{0,2,1:T(8,128)(2,1)} %bitcast.162, bf16[512,3,32]{0,2,1:T(8,128)(2,1)S(1)} %get-tuple-element.336, bf16[512,3,32]{0,2,1:T(8,128)(2,1)S(1)} %get-tuple-element.335), kind=kOutput, calls=%fused_computation.16 | convolution fusion | flops 824572416 | bytes 29038592 | tf_op jit(solution)/shard_map/qhd,khd->hqk/dot_general | solution.py:87
  120.4 12.0 %fusion.8 = f32[3,512]{1,0:T(4,128)S(1)} fusion(f32[3,512,4096]{2,1,0:T(8,128)} %get-tuple-element.347, f32[3,512]{1,0:T(4,128)S(1)} %broadcast_maximum_fusion, pred[512,4096]{1,0:T(8,128)(4,1)S(1)} %broadcast_compare_fusion.1), kind=kLoop, calls=%fused_computation.17 | loop fusion | flops 25164288 | bytes 27275264 | tf_op jit(solution)/shard_map/reduce_sum | solution.py:166
  132.4 21.2 %all-gather.12.cloned.1.call-done = bf16[4096,1,192]{0,2,1:T(8,128)(2,1)} async-done(((bf16[512,1,192]{0,2,1:T(8,128)(2,1)}), bf16[4096,1,192]{0,2,1:T(8,128)(2,1)}) %all-gather.12.cloned.1.call-update) | async-done | bytes 1572880 | tf_op jit(solution)/shard_map/all_gather | solution.py:160
  153.6 12.0 %fusion.29 = (bf16[512,3,64]{0,2,1:T(8,128)(2,1)S(1)}, f32[3,512,64]{1,2,0:T(8,128)}) fusion(f32[512,3]{0,1:T(4,128)S(1)} %bitcast.183, bf16[4096,3,64]{0,2,1:T(8,128)(2,1)} %bitcast.163, f32[3,512,4096]{2,1,0:T(8,128)} %get-tuple-element.347, f32[3,512]{1,0:T(4,128)S(1)} %broadcast_maximum_fusion, pred[512,4096]{1,0:T(8,128)(4,1)S(1)} %broadcast_compare_fusion.1), kind=kOutput, calls=%fused_computation.58 | convolution fusion | flops 830668800 | bytes 29437952 | tf_op jit(solution)/shard_map/hqk,khd->hqd/dot_general | solution.py:167
  169.4 19.2 %reduce-scatter.15.cloned.1.call-done = bf16[128,768]{1,0:T(8,128)(2,1)} async-done(((bf16[512,768]{1,0:T(8,128)(2,1)}), bf16[128,768]{1,0:T(8,128)(2,1)}) %reduce-scatter.15.cloned.1.call-update) | async-done | bytes 196624 | tf_op jit(solution)/shard_map/reduce_scatter | solution.py:77
  191.8 8.4 all_gather.37
  200.2 43.2 %all-gather.8.cloned.1.call-done = bf16[768,2,768]{2,0,1:T(8,128)(2,1)} async-done(((bf16[96,2,768]{2,0,1:T(8,128)(2,1)}), bf16[768,2,768]{2,0,1:T(8,128)(2,1)}) %all-gather.8.cloned.1.call-update) | async-done | bytes 2359312 | tf_op jit(solution)/shard_map/all_gather | solution.py:136
  248.6 36.7 %all-gather.10.cloned.1.call-done = bf16[768,768]{0,1:T(8,128)(2,1)} async-done(((bf16[768,96]{0,1:T(8,128)(2,1)}), bf16[768,768]{0,1:T(8,128)(2,1)}) %all-gather.10.cloned.1.call-update) | async-done | bytes 1179664 | tf_op jit(solution)/shard_map/all_gather | solution.py:137
  288.3 22.1 %reduce-scatter.17.cloned.1.call-done = bf16[128,768]{1,0:T(8,128)(2,1)} async-done(((bf16[512,768]{1,0:T(8,128)(2,1)}), bf16[128,768]{1,0:T(8,128)(2,1)}) %reduce-scatter.17.cloned.1.call-update) | async-done | bytes 196624 | tf_op jit(solution)/shard_map/reduce_scatter | solution.py:77
  313.7 8.2 all_gather.40
  328.2 23.7 %reduce-scatter.19.cloned.1.call-done = bf16[128,768]{1,0:T(8,128)(2,1)} async-done(((bf16[512,768]{1,0:T(8,128)(2,1)}), bf16[128,768]{1,0:T(8,128)(2,1)}) %reduce-scatter.19.cloned.1.call-update) | async-done | bytes 196624 | tf_op jit(solution)/shard_map/reduce_scatter | solution.py:77
  368.2 58.9 %while.18 = (s32[]{:T(128)}, f32[512,3,64]{0,2,1:T(8,128)S(1)}, f32[4096,192]{0,1:T(8,128)}, f32[4096,192]{0,1:T(8,128)}, bf16[4096,192]{0,1:T(8,128)(2,1)S(1)},...) while((s32[]{:T(128)}, f32[512,3,64]{0,2,1:T(8,128)S(1)}, ...), condition=%wide.region_18.19_spmd.clone, body=%wide.region_17.18_spmd.clone.sunk | while | flops 2045968384 | bytes 107786520 | solution.py:274
  434.6 68.0 %reduce-scatter.21.cloned.1.call-done = f32[512,192]{0,1:T(8,128)} async-done(((f32[4096,192]{0,1:T(8,128)}), f32[512,192]{0,1:T(8,128)}) %reduce-scatter.21.cloned.1.call-update) | async-done | bytes 393232 | tf_op jit(solution)/shard_map/reduce_scatter | solution.py:278
  503.8 76.9 %reduce-scatter.23.cloned.1.call-done = f32[512,192]{0,1:T(8,128)} async-done(((f32[4096,192]{0,1:T(8,128)}), f32[512,192]{0,1:T(8,128)}) %reduce-scatter.23.cloned.1.call-update) | async-done | bytes 393232 | tf_op jit(solution)/shard_map/reduce_scatter | solution.py:279
  590.5 40.1 %all-reduce = (f32[768]{0:T(1024)}, f32[768]{0:T(1024)}, f32[768]{0:T(1024)}, f32[768]{0:T(1024)}) all-reduce(f32[768]{0:T(1024)S(1)} %get-tuple-element.283, f32[768]{0:T(1024)S(1)} %get-tuple-element.288, f32[768]{0:T(1024)S(1)} %copy-done.34, f32[768]{0:T(1024)S(1)} %copy-done.35), channel_id=1, replica_groups=mesh['row'=8,'col'=4] {'row','col'}, use_global_device_ids=true, to_apply=%region_27.28 | all-reduce | flops 3072 | bytes 24576 | tf_op jit(solution)/shard_map/psum | solution.py:302
  630.6 15.3 %reduce-scatter.33.cloned.1.call-done = f32[96,192]{1,0:T(8,128)} async-done(((f32[768,192]{1,0:T(8,128)}), f32[96,192]{1,0:T(8,128)}) %reduce-scatter.33.cloned.1.call-update) | async-done | bytes 73744
  647.6 96.2 %reduce-scatter.27.cloned.1.call-done = f32[96,2,768]{2,0,1:T(8,128)} async-done(((f32[768,2,768]{2,0,1:T(8,128)}), f32[96,2,768]{2,0,1:T(8,128)}) %reduce-scatter.27.cloned.1.call-update) | async-done | bytes 589840 | tf_op jit(solution)/shard_map/reduce_scatter | solution.py:299
  746.1 23.1 %reduce-scatter.25.cloned.1.call-done = bf16[128,768]{1,0:T(8,128)(2,1)} async-done(((bf16[512,768]{1,0:T(8,128)(2,1)}), bf16[128,768]{1,0:T(8,128)(2,1)}) %reduce-scatter.25.cloned.1.call-update) | async-done | bytes 196624 | tf_op jit(solution)/shard_map/reduce_scatter | solution.py:77
  771.0 69.1 %reduce-scatter.31.cloned.1.call-done = f32[96,576]{1,0:T(8,128)} async-done(((f32[768,576]{1,0:T(8,128)}), f32[96,576]{1,0:T(8,128)}) %reduce-scatter.31.cloned.1.call-update) | async-done | bytes 221200
  842.0 69.8 %reduce-scatter.29.cloned.1.call-done = f32[768,96]{0,1:T(8,128)} async-done(((f32[768,768]{0,1:T(8,128)}), f32[768,96]{0,1:T(8,128)}) %reduce-scatter.29.cloned.1.call-update) | async-done | bytes 294928 | tf_op jit(solution)/shard_map/reduce_scatter | solution.py:300
  (200 shorter events, 134.8 us)
Async XLA Ops:
  7.2 100.7 %all-gather.6.cloned.1.call-start = ((), (), s32[]{:S(2)}) async-start(), calls=%async_computation.10 | async-start | bytes 1769472 | tf_op jit(solution)/shard_map/all_gather | solution.py:159
  62.0 91.6 %all-gather.12.cloned.1.call-start = ((), (), s32[]{:S(2)}) async-start(), calls=%async_computation.21 | async-start | bytes 1769472 | tf_op jit(solution)/shard_map/all_gather | solution.py:160
  62.7 125.8 %reduce-scatter.15.cloned.1.call-start = ((), (), s32[]{:S(2)}) async-start(), calls=%async_computation.11 | async-start | bytes 983040 | tf_op jit(solution)/shard_map/reduce_scatter | solution.py:77
  167.0 76.4 %all-gather.8.cloned.1.call-start = ((), (), s32[]{:S(2)}) async-start(), calls=%async_computation.12 | async-start | bytes 2654208 | tf_op jit(solution)/shard_map/all_gather | solution.py:136
  168.8 116.5 %all-gather.10.cloned.1.call-start = ((), (), s32[]{:S(2)}) async-start(), calls=%async_computation.13 | async-start | bytes 1327104 | tf_op jit(solution)/shard_map/all_gather | solution.py:137
  169.3 141.1 %reduce-scatter.17.cloned.1.call-start = ((), (), s32[]{:S(2)}) async-start(), calls=%async_computation.14 | async-start | bytes 983040 | tf_op jit(solution)/shard_map/reduce_scatter | solution.py:77
  248.6 64.2 %copy-start.7 = (bf16[512,768]{1,0:T(8,128)(2,1)}, bf16[512,768]{1,0:T(8,128)(2,1)S(1)}, u32[]{:S(2)}) copy-start(bf16[512,768]{1,0:T(8,128)(2,1)S(1)} %multiply_convert_fusion.2) | copy-start | bytes 2359300
  248.6 63.4 %copy-start.20 = (bf16[128,768]{1,0:T(8,128)(2,1)S(1)}, bf16[128,768]{1,0:T(8,128)(2,1)}, u32[]{:S(2)}) copy-start(bf16[128,768]{1,0:T(8,128)(2,1)} %param.23) | copy-start | bytes 589828
  248.6 64.2 %copy-start.36 = (f32[768]{0:T(1024)S(1)}, f32[768]{0:T(1024)}, u32[]{:S(2)}) copy-start(f32[768]{0:T(1024)} %param.22) | copy-start | bytes 9220
  288.3 63.7 %reduce-scatter.19.cloned.1.call-start = ((), (), s32[]{:S(2)}) async-start(), calls=%async_computation.15 | async-start | bytes 983040 | tf_op jit(solution)/shard_map/reduce_scatter | solution.py:77
  328.1 174.4 %reduce-scatter.21.cloned.1.call-start = ((), (), s32[]{:S(2)}) async-start(), calls=%async_computation.16 | async-start | bytes 3538944 | tf_op jit(solution)/shard_map/reduce_scatter | solution.py:278
  427.2 153.5 %reduce-scatter.23.cloned.1.call-start = ((), (), s32[]{:S(2)}) async-start(), calls=%async_computation.17 | async-start | bytes 3538944 | tf_op jit(solution)/shard_map/reduce_scatter | solution.py:279
  427.9 218.0 %reduce-scatter.33.cloned.1.call-start = ((), (), s32[]{:S(2)}) async-start(), calls=%async_computation.23 | async-start | bytes 884736
  429.7 314.1 %reduce-scatter.27.cloned.1.call-start = ((), (), s32[]{:S(2)}) async-start(), calls=%async_computation.19 | async-start | bytes 5308416 | tf_op jit(solution)/shard_map/reduce_scatter | solution.py:299
  434.5 69.1 %copy-start.22 = (f32[512,32]{0,1:T(8,128)S(1)}, f32[512,32]{0,1:T(8,128)}, u32[]{:S(2)}) copy-start(f32[512,32]{0,1:T(8,128)} %copy-done.21) | copy-start | bytes 196612
  434.5 69.1 %copy-start.24 = (f32[512,32]{0,1:T(8,128)S(1)}, f32[512,32]{0,1:T(8,128)}, u32[]{:S(2)}) copy-start(f32[512,32]{0,1:T(8,128)} %copy-done.23) | copy-start | bytes 196612
  434.5 147.9 %copy-start.10 = (bf16[768,3,192]{0,2,1:T(8,128)(2,1)S(1)}, bf16[768,3,192]{0,2,1:T(8,128)(2,1)}, u32[]{:S(2)}) copy-start(bf16[768,3,192]{0,2,1:T(8,128)(2,1)} %copy-done.9) | copy-start | bytes 2654212
  434.5 334.8 %reduce-scatter.25.cloned.1.call-start = ((), (), s32[]{:S(2)}) async-start(), calls=%async_computation.18 | async-start | bytes 983040 | tf_op jit(solution)/shard_map/reduce_scatter | solution.py:77
  503.7 80.4 %copy-start.26 = (bf16[512,3,64]{0,2,1:T(8,128)(2,1)}, bf16[512,3,64]{0,2,1:T(8,128)(2,1)S(1)}, u32[]{:S(2)}) copy-start(bf16[512,3,64]{0,2,1:T(8,128)(2,1)S(1)} %pad_maximum_fusion.8) | copy-start | bytes 589828
  503.8 80.7 %copy-start.14 = (bf16[512,768]{1,0:T(8,128)(2,1)S(1)}, bf16[512,768]{1,0:T(8,128)(2,1)}, u32[]{:S(2)}) copy-start(bf16[512,768]{1,0:T(8,128)(2,1)} %copy-done.13) | copy-start | bytes 2359300
  503.8 80.4 %copy-start.27 = (bf16[512,3,64]{0,2,1:T(8,128)(2,1)}, bf16[512,3,64]{0,2,1:T(8,128)(2,1)S(1)}, u32[]{:S(2)}) copy-start(bf16[512,3,64]{0,2,1:T(8,128)(2,1)S(1)} %pad_maximum_fusion.9) | copy-start | bytes 589828
  584.2 255.8 %reduce-scatter.31.cloned.1.call-start = ((), (), s32[]{:S(2)}) async-start(), calls=%async_computation.22 | async-start | bytes 2211840
  588.1 323.7 %reduce-scatter.29.cloned.1.call-start = ((), (), s32[]{:S(2)}) async-start(), calls=%async_computation.20 | async-start | bytes 2654208 | tf_op jit(solution)/shard_map/reduce_scatter | solution.py:300
  590.5 178.8 %copy-start.17 = (f32[128,768]{1,0:T(8,128)S(1)}, f32[128,768]{1,0:T(8,128)}, u32[]{:S(2)}) copy-start(f32[128,768]{1,0:T(8,128)} %get-tuple-element.320) | copy-start | bytes 1179652
  (33 other events, 386.7 us)
Sparse Core Ops, SparseCore 0:
  62.1 45.7 all-gather.5
  110.5 43.0 all-gather.11
  167.1 21.4 reduce-scatter.14
  191.4 51.9 all-gather.7
  245.7 39.5 all-gather.9
  288.4 22.0 reduce-scatter.16
  328.3 23.6 reduce-scatter.18
  427.3 75.2 reduce-scatter.20
  506.6 74.0 reduce-scatter.22
  584.2 61.6 reduce-scatter.32
  649.6 94.1 reduce-scatter.26
  746.2 23.0 reduce-scatter.24
  773.1 66.8 reduce-scatter.30
  843.9 67.8 reduce-scatter.28
where the time goes:
time: 919 us; the launch traced here: 918 us
  waiting for transfers between devices  598 us (65%)
  blocking collectives  144 us (16%)
  matrix products  101 us (11%)
  other arithmetic  31.8 us (3%)
  local copies, waits for them, and re-layouts  27.6 us (3%)
  between operations  14.5 us (2%)
    reduce_scatter x1, waiting for transfers between devices, local(): lax.psum_scatter(grad_wgu, 'row', scatter_dimension=0, tiled=True)  96.2 us
    reduce_scatter x4, waiting for transfers between devices, column_sum(): lax.psum_scatter(product(left).astype(jnp.bfloat16), 'col', scatter_dimen...  88.2 us
    unnamed x16, waiting for transfers between devices  85.8 us
    reduce_scatter x1, waiting for transfers between devices, local(): lax.psum_scatter(grad_values_all, 'row', scatter_dimension=0, tiled=True)  76.9 us
    reduce_scatter x1, waiting for transfers between devices, local(): lax.psum_scatter(grad_down, 'row', scatter_dimension=1, tiled=True)  69.8 us
    reduce_scatter x1, waiting for transfers between devices, local(): lax.psum_scatter(grad_keys_all, 'row', scatter_dimension=0, tiled=True)  68 us
    all_gather x1, waiting for transfers between devices, local(): lax.all_gather(w_gate_up, 'row', axis=0, tiled=True)  43.2 us
    psum x1, blocking collectives, local(): lax.psum((grad_gain1, grad_bias1, grad_gain2, grad_bias2), ('row', 'col'))  40.1 us
  transfers between devices with their start and end apart: 14, of which 14 were waited for; matrix products, arithmetic and copies ran while one was open for 6% of the time, Pallas kernels for 0%

commit v1 on v0

--- a/solution.py
+++ b/solution.py
@@ -132,7 +132,9 @@
     shards = lax.axis_size("row")
     full_qkv, full_out, full_gate_up, full_down = (
         lax.all_gather(w_qkv, "row", axis=0, tiled=True),
-        lax.all_gather(w_out, "row", axis=1, tiled=True),
+        jnp.concatenate(
+            lax.all_to_all(jnp.stack([w_out] * lax.axis_size("row")), "row", 0, 0), axis=1
+        ),
         lax.all_gather(w_gate_up, "row", axis=0, tiled=True),
         lax.all_gather(w_down, "row", axis=1, tiled=True),
     )

time: 919 us -> 922 us (level)
  blocking collectives: 144 us -> 112 us
  waiting for transfers between devices: 598 us -> 628 us
    all_gather x1 -> x0, blocking collectives: 31.8 us -> none  [local(): lax.all_gather(w_out, 'row', axis=1, tiled=True)]
    all_to_all x0 -> x1, waiting for transfers between devices: none -> 15.9 us  [local(): lax.all_to_all(jnp.stack([w_out] * lax.axis_size('row')), 'row', 0, 0)]
    all_gather x1, waiting for transfers between devices: 11.8 us -> 24 us  [local(): key_piece = lax.all_gather(key_bf, 'row', axis=0, tiled=True)]
  transfers between devices with their start and end apart: 14 -> 15, of which waited for: 14 -> 15; matrix products, arithmetic and copies ran while one was open for 6% -> 6% of each run, Pallas kernels for 0% -> 0%
where the time goes in v1:
time: 922 us; the launch traced here: 920 us
  waiting for transfers between devices  628 us (68%)
  blocking collectives  112 us (12%)
  matrix products  102 us (11%)
  other arithmetic  31.8 us (3%)
  local copies, waits for them, and re-layouts  27.9 us (3%)
  between operations  14.6 us (2%)
    reduce_scatter x1, waiting for transfers between devices, local(): lax.psum_scatter(grad_wgu, 'row', scatter_dimension=0, tiled=True)  96.5 us
    reduce_scatter x4, waiting for transfers between devices, column_sum(): lax.psum_scatter(product(left).astype(jnp.bfloat16), 'col', scatter_dimen...  89.1 us
    unnamed x16, waiting for transfers between devices  85.8 us
    reduce_scatter x1, waiting for transfers between devices, local(): lax.psum_scatter(grad_values_all, 'row', scatter_dimension=0, tiled=True)  77 us
    reduce_scatter x1, waiting for transfers between devices, local(): lax.psum_scatter(grad_down, 'row', scatter_dimension=1, tiled=True)  69.8 us
    reduce_scatter x1, waiting for transfers between devices, local(): lax.psum_scatter(grad_keys_all, 'row', scatter_dimension=0, tiled=True)  68.1 us
    all_gather x1, waiting for transfers between devices, local(): lax.all_gather(w_gate_up, 'row', axis=0, tiled=True)  43.2 us
    psum x1, blocking collectives, local(): lax.psum((grad_gain1, grad_bias1, grad_gain2, grad_bias2), ('row', 'col'))  40 us
  transfers between devices with their start and end apart: 15, of which 15 were waited for; matrix products, arithmetic and copies ran while one was open for 6% of the time, Pallas kernels for 0%

profile of v1, /device:TPU:0, one launch (start us, length us, event | category | flops | bytes accessed | tf_op | source)
XLA Modules:
  0.0 920.5 jit_solution(11304103595296093286)
XLA Ops:
  9.8 38.8 %all_gather.30 = bf16[768,3,192]{2,1,0:T(4,128)(2,1)S(1)} all-gather(bf16[96,3,192]{2,1,0:T(4,128)(2,1)S(1)} %copy.54), channel_id=1, replica_groups=mesh['row'=8,'col'=4] {'row'}, dimensions={0}, use_global_device_ids=true | all-gather | bytes 995328 | tf_op jit(solution)/shard_map/all_gather | solution.py:134
  49.5 8.8 all_gather.29
  68.7 15.9 %all-to-all-done = bf16[8,192,96]{2,1,0:T(8,128)(2,1)S(1)} async-done(((bf16[8,192,96]{2,1,0:T(8,128)(2,1)}), bf16[8,192,96]{2,1,0:T(8,128)(2,1)S(1)}, u32[]{:S(2)}, u32[]{:S(2)}) %all-to-all-start) | async-done | bytes 294944 | tf_op jit(solution)/shard_map/all_to_all | solution.py:136
  85.2 24.0 %all-gather.6.cloned.1.call-done = bf16[4096,192]{0,1:T(8,128)(2,1)} async-done(((bf16[512,192]{0,1:T(8,128)(2,1)}), bf16[4096,192]{0,1:T(8,128)(2,1)}) %all-gather.6.cloned.1.call-update) | async-done | bytes 1572880 | tf_op jit(solution)/shard_map/all_gather | solution.py:161
  109.3 12.6 %select_reduce_fusion = (f32[3,512]{1,0:T(4,128)S(1)}, f32[3,512,4096]{2,1,0:T(8,128)}) fusion(pred[512,4096]{1,0:T(8,128)(4,1)S(1)} %broadcast_compare_fusion.1, bf16[4096,3,64]{0,2,1:T(8,128)(2,1)} %bitcast.163, bf16[512,3,32]{0,2,1:T(8,128)(2,1)S(1)} %get-tuple-element.346, bf16[512,3,32]{0,2,1:T(8,128)(2,1)S(1)} %get-tuple-element.345), kind=kOutput, calls=%fused_computation.16 | convolution fusion | flops 824572416 | bytes 29038592 | tf_op jit(solution)/shard_map/qhd,khd->hqk/dot_general | solution.py:87
  121.9 12.0 %fusion.8 = f32[3,512]{1,0:T(4,128)S(1)} fusion(f32[3,512,4096]{2,1,0:T(8,128)} %get-tuple-element.357, f32[3,512]{1,0:T(4,128)S(1)} %broadcast_maximum_fusion, pred[512,4096]{1,0:T(8,128)(4,1)S(1)} %broadcast_compare_fusion.1), kind=kLoop, calls=%fused_computation.17 | loop fusion | flops 25164288 | bytes 27275264 | tf_op jit(solution)/shard_map/reduce_sum | solution.py:168
  133.8 21.6 %all-gather.12.cloned.1.call-done = bf16[4096,1,192]{0,2,1:T(8,128)(2,1)} async-done(((bf16[512,1,192]{0,2,1:T(8,128)(2,1)}), bf16[4096,1,192]{0,2,1:T(8,128)(2,1)}) %all-gather.12.cloned.1.call-update) | async-done | bytes 1572880 | tf_op jit(solution)/shard_map/all_gather | solution.py:162
  155.4 12.1 %fusion.29 = (bf16[512,3,64]{0,2,1:T(8,128)(2,1)S(1)}, f32[3,512,64]{1,2,0:T(8,128)}) fusion(f32[512,3]{0,1:T(4,128)S(1)} %bitcast.185, bf16[4096,3,64]{0,2,1:T(8,128)(2,1)} %bitcast.164, f32[3,512,4096]{2,1,0:T(8,128)} %get-tuple-element.357, f32[3,512]{1,0:T(4,128)S(1)} %broadcast_maximum_fusion, pred[512,4096]{1,0:T(8,128)(4,1)S(1)} %broadcast_compare_fusion.1), kind=kOutput, calls=%fused_computation.58 | convolution fusion | flops 830668800 | bytes 29437952 | tf_op jit(solution)/shard_map/hqk,khd->hqd/dot_general | solution.py:169
  170.3 20.1 %reduce-scatter.15.cloned.1.call-done = bf16[128,768]{1,0:T(8,128)(2,1)} async-done(((bf16[512,768]{1,0:T(8,128)(2,1)}), bf16[128,768]{1,0:T(8,128)(2,1)}) %reduce-scatter.15.cloned.1.call-update) | async-done | bytes 196624 | tf_op jit(solution)/shard_map/reduce_scatter | solution.py:77
  193.7 8.4 all_gather.33
  202.1 43.2 %all-gather.8.cloned.1.call-done = bf16[768,2,768]{2,0,1:T(8,128)(2,1)} async-done(((bf16[96,2,768]{2,0,1:T(8,128)(2,1)}), bf16[768,2,768]{2,0,1:T(8,128)(2,1)}) %all-gather.8.cloned.1.call-update) | async-done | bytes 2359312 | tf_op jit(solution)/shard_map/all_gather | solution.py:138
  250.5 36.7 %all-gather.10.cloned.1.call-done = bf16[768,768]{0,1:T(8,128)(2,1)} async-done(((bf16[768,96]{0,1:T(8,128)(2,1)}), bf16[768,768]{0,1:T(8,128)(2,1)}) %all-gather.10.cloned.1.call-update) | async-done | bytes 1179664 | tf_op jit(solution)/shard_map/all_gather | solution.py:139
  290.2 22.1 %reduce-scatter.17.cloned.1.call-done = bf16[128,768]{1,0:T(8,128)(2,1)} async-done(((bf16[512,768]{1,0:T(8,128)(2,1)}), bf16[128,768]{1,0:T(8,128)(2,1)}) %reduce-scatter.17.cloned.1.call-update) | async-done | bytes 196624 | tf_op jit(solution)/shard_map/reduce_scatter | solution.py:77
  315.6 8.2 all_gather.36
  330.2 23.7 %reduce-scatter.19.cloned.1.call-done = bf16[128,768]{1,0:T(8,128)(2,1)} async-done(((bf16[512,768]{1,0:T(8,128)(2,1)}), bf16[128,768]{1,0:T(8,128)(2,1)}) %reduce-scatter.19.cloned.1.call-update) | async-done | bytes 196624 | tf_op jit(solution)/shard_map/reduce_scatter | solution.py:77
  370.2 58.8 %while.18 = (s32[]{:T(128)}, f32[512,3,64]{0,2,1:T(8,128)S(1)}, f32[4096,192]{0,1:T(8,128)}, f32[4096,192]{0,1:T(8,128)}, bf16[4096,192]{0,1:T(8,128)(2,1)S(1)},...) while((s32[]{:T(128)}, f32[512,3,64]{0,2,1:T(8,128)S(1)}, ...), condition=%wide.region_18.19_spmd.clone, body=%wide.region_17.18_spmd.clone.sunk | while | flops 2045968384 | bytes 107786520 | solution.py:276
  436.4 68.1 %reduce-scatter.21.cloned.1.call-done = f32[512,192]{0,1:T(8,128)} async-done(((f32[4096,192]{0,1:T(8,128)}), f32[512,192]{0,1:T(8,128)}) %reduce-scatter.21.cloned.1.call-update) | async-done | bytes 393232 | tf_op jit(solution)/shard_map/reduce_scatter | solution.py:280
  505.8 77.0 %reduce-scatter.23.cloned.1.call-done = f32[512,192]{0,1:T(8,128)} async-done(((f32[4096,192]{0,1:T(8,128)}), f32[512,192]{0,1:T(8,128)}) %reduce-scatter.23.cloned.1.call-update) | async-done | bytes 393232 | tf_op jit(solution)/shard_map/reduce_scatter | solution.py:281
  592.6 40.0 %all-reduce = (f32[768]{0:T(1024)}, f32[768]{0:T(1024)}, f32[768]{0:T(1024)}, f32[768]{0:T(1024)}) all-reduce(f32[768]{0:T(1024)S(1)} %get-tuple-element.293, f32[768]{0:T(1024)S(1)} %get-tuple-element.298, f32[768]{0:T(1024)S(1)} %copy-done.35, f32[768]{0:T(1024)S(1)} %copy-done.36), channel_id=1, replica_groups=mesh['row'=8,'col'=4] {'row','col'}, use_global_device_ids=true, to_apply=%region_27.28 | all-reduce | flops 3072 | bytes 24576 | tf_op jit(solution)/shard_map/psum | solution.py:304
  632.5 15.5 %reduce-scatter.33.cloned.1.call-done = f32[96,192]{1,0:T(8,128)} async-done(((f32[768,192]{1,0:T(8,128)}), f32[96,192]{1,0:T(8,128)}) %reduce-scatter.33.cloned.1.call-update) | async-done | bytes 73744
  649.6 96.5 %reduce-scatter.27.cloned.1.call-done = f32[96,2,768]{2,0,1:T(8,128)} async-done(((f32[768,2,768]{2,0,1:T(8,128)}), f32[96,2,768]{2,0,1:T(8,128)}) %reduce-scatter.27.cloned.1.call-update) | async-done | bytes 589840 | tf_op jit(solution)/shard_map/reduce_scatter | solution.py:301
  748.4 23.1 %reduce-scatter.25.cloned.1.call-done = bf16[128,768]{1,0:T(8,128)(2,1)} async-done(((bf16[512,768]{1,0:T(8,128)(2,1)}), bf16[128,768]{1,0:T(8,128)(2,1)}) %reduce-scatter.25.cloned.1.call-update) | async-done | bytes 196624 | tf_op jit(solution)/shard_map/reduce_scatter | solution.py:77
  773.2 68.9 %reduce-scatter.31.cloned.1.call-done = f32[96,576]{1,0:T(8,128)} async-done(((f32[768,576]{1,0:T(8,128)}), f32[96,576]{1,0:T(8,128)}) %reduce-scatter.31.cloned.1.call-update) | async-done | bytes 221200
  844.1 69.8 %reduce-scatter.29.cloned.1.call-done = f32[768,96]{0,1:T(8,128)} async-done(((f32[768,768]{0,1:T(8,128)}), f32[768,96]{0,1:T(8,128)}) %reduce-scatter.29.cloned.1.call-update) | async-done | bytes 294928 | tf_op jit(solution)/shard_map/reduce_scatter | solution.py:302
  (205 shorter events, 138.8 us)
Async XLA Ops:
  7.2 102.1 %all-gather.6.cloned.1.call-start = ((), (), s32[]{:S(2)}) async-start(), calls=%async_computation.11 | async-start | bytes 1769472 | tf_op jit(solution)/shard_map/all_gather | solution.py:161
  62.8 21.9 %all-to-all-start = ((bf16[8,192,96]{2,1,0:T(8,128)(2,1)}), bf16[8,192,96]{2,1,0:T(8,128)(2,1)S(1)}, u32[]{:S(2)}, u32[]{:S(2)}) async-start(bf16[8,192,96]{2,1,0:T(8,128)(2,1)} %stack.31), calls=%async_computation | async-start | bytes 786432 | tf_op jit(solution)/shard_map/all_to_all | solution.py:136
  66.5 88.9 %all-gather.12.cloned.1.call-start = ((), (), s32[]{:S(2)}) async-start(), calls=%async_computation.22 | async-start | bytes 1769472 | tf_op jit(solution)/shard_map/all_gather | solution.py:162
  67.3 123.2 %reduce-scatter.15.cloned.1.call-start = ((), (), s32[]{:S(2)}) async-start(), calls=%async_computation.12 | async-start | bytes 983040 | tf_op jit(solution)/shard_map/reduce_scatter | solution.py:77
  168.9 76.4 %all-gather.8.cloned.1.call-start = ((), (), s32[]{:S(2)}) async-start(), calls=%async_computation.13 | async-start | bytes 2654208 | tf_op jit(solution)/shard_map/all_gather | solution.py:138
  169.7 117.5 %all-gather.10.cloned.1.call-start = ((), (), s32[]{:S(2)}) async-start(), calls=%async_computation.14 | async-start | bytes 1327104 | tf_op jit(solution)/shard_map/all_gather | solution.py:139
  170.3 142.1 %reduce-scatter.17.cloned.1.call-start = ((), (), s32[]{:S(2)}) async-start(), calls=%async_computation.15 | async-start | bytes 983040 | tf_op jit(solution)/shard_map/reduce_scatter | solution.py:77
  250.5 64.2 %copy-start.7 = (bf16[512,768]{1,0:T(8,128)(2,1)}, bf16[512,768]{1,0:T(8,128)(2,1)S(1)}, u32[]{:S(2)}) copy-start(bf16[512,768]{1,0:T(8,128)(2,1)S(1)} %multiply_convert_fusion.2) | copy-start | bytes 2359300
  250.5 64.2 %copy-start.37 = (f32[768]{0:T(1024)S(1)}, f32[768]{0:T(1024)}, u32[]{:S(2)}) copy-start(f32[768]{0:T(1024)} %param.22) | copy-start | bytes 9220
  290.2 63.7 %reduce-scatter.19.cloned.1.call-start = ((), (), s32[]{:S(2)}) async-start(), calls=%async_computation.16 | async-start | bytes 983040 | tf_op jit(solution)/shard_map/reduce_scatter | solution.py:77
  330.1 174.4 %reduce-scatter.21.cloned.1.call-start = ((), (), s32[]{:S(2)}) async-start(), calls=%async_computation.17 | async-start | bytes 3538944 | tf_op jit(solution)/shard_map/reduce_scatter | solution.py:280
  429.0 153.7 %reduce-scatter.23.cloned.1.call-start = ((), (), s32[]{:S(2)}) async-start(), calls=%async_computation.18 | async-start | bytes 3538944 | tf_op jit(solution)/shard_map/reduce_scatter | solution.py:281
  429.8 218.2 %reduce-scatter.33.cloned.1.call-start = ((), (), s32[]{:S(2)}) async-start(), calls=%async_computation.24 | async-start | bytes 884736
  431.6 314.5 %reduce-scatter.27.cloned.1.call-start = ((), (), s32[]{:S(2)}) async-start(), calls=%async_computation.20 | async-start | bytes 5308416 | tf_op jit(solution)/shard_map/reduce_scatter | solution.py:301
  436.3 69.2 %copy-start.22 = (f32[512,32]{0,1:T(8,128)S(1)}, f32[512,32]{0,1:T(8,128)}, u32[]{:S(2)}) copy-start(f32[512,32]{0,1:T(8,128)} %copy-done.21) | copy-start | bytes 196612
  436.3 69.2 %copy-start.24 = (f32[512,32]{0,1:T(8,128)S(1)}, f32[512,32]{0,1:T(8,128)}, u32[]{:S(2)}) copy-start(f32[512,32]{0,1:T(8,128)} %copy-done.23) | copy-start | bytes 196612
  436.3 148.1 %copy-start.10 = (bf16[768,3,192]{0,2,1:T(8,128)(2,1)S(1)}, bf16[768,3,192]{0,2,1:T(8,128)(2,1)}, u32[]{:S(2)}) copy-start(bf16[768,3,192]{0,2,1:T(8,128)(2,1)} %copy-done.9) | copy-start | bytes 2654212
  436.3 335.2 %reduce-scatter.25.cloned.1.call-start = ((), (), s32[]{:S(2)}) async-start(), calls=%async_computation.19 | async-start | bytes 983040 | tf_op jit(solution)/shard_map/reduce_scatter | solution.py:77
  505.7 80.5 %copy-start.27 = (bf16[512,3,64]{0,2,1:T(8,128)(2,1)}, bf16[512,3,64]{0,2,1:T(8,128)(2,1)S(1)}, u32[]{:S(2)}) copy-start(bf16[512,3,64]{0,2,1:T(8,128)(2,1)S(1)} %pad_maximum_fusion.8) | copy-start | bytes 589828
  505.7 80.8 %copy-start.14 = (bf16[512,768]{1,0:T(8,128)(2,1)S(1)}, bf16[512,768]{1,0:T(8,128)(2,1)}, u32[]{:S(2)}) copy-start(bf16[512,768]{1,0:T(8,128)(2,1)} %copy-done.13) | copy-start | bytes 2359300
  505.7 80.5 %copy-start.28 = (bf16[512,3,64]{0,2,1:T(8,128)(2,1)}, bf16[512,3,64]{0,2,1:T(8,128)(2,1)S(1)}, u32[]{:S(2)}) copy-start(bf16[512,3,64]{0,2,1:T(8,128)(2,1)S(1)} %pad_maximum_fusion.9) | copy-start | bytes 589828
  586.2 255.9 %reduce-scatter.31.cloned.1.call-start = ((), (), s32[]{:S(2)}) async-start(), calls=%async_computation.23 | async-start | bytes 2211840
  590.2 323.8 %reduce-scatter.29.cloned.1.call-start = ((), (), s32[]{:S(2)}) async-start(), calls=%async_computation.21 | async-start | bytes 2654208 | tf_op jit(solution)/shard_map/reduce_scatter | solution.py:302
  592.5 179.0 %copy-start.17 = (f32[128,768]{1,0:T(8,128)S(1)}, f32[128,768]{1,0:T(8,128)}, u32[]{:S(2)}) copy-start(f32[128,768]{1,0:T(8,128)} %get-tuple-element.330) | copy-start | bytes 1179652
  (35 other events, 462.1 us)
Sparse Core Ops, SparseCore 0:
  62.1 47.1 all-gather.5
  111.9 43.5 all-gather.11
  169.0 21.4 reduce-scatter.14
  193.3 51.9 all-gather.7
  247.6 39.5 all-gather.9
  290.3 22.0 reduce-scatter.16
  330.2 23.6 reduce-scatter.18
  429.1 75.3 reduce-scatter.20
  508.5 74.1 reduce-scatter.22
  586.3 61.6 reduce-scatter.32
  651.6 94.4 reduce-scatter.26
  748.5 23.0 reduce-scatter.24
  775.4 66.6 reduce-scatter.30
  846.1 67.8 reduce-scatter.28
